TPU v7x, 32 devices: a whole 2x2x4 slice. The times are simulated.
32 devices in a mesh: rows: 4 (over x, core), cols: 8 (over z, y).
Axes of the slice: x: 2, y: 2, z: 4, core: 2. Of those that a mesh axis runs over, the one named last changes fastest.
Arguments:
- image: bfloat16 [48, 64, 2048], P(None, 'rows', 'cols'), may hold values from -6 to 6
- perturb: float32 [48, 64, 2048], P(None, 'rows', 'cols'), may hold values from -0.5 to 0.5
- target: bfloat16 [48, 32, 1024], P(None, 'rows', 'cols'), may hold values from -6 to 6
- kernel_one: float32 [48, 48, 3, 3], replicated, may hold values from -0.3125 to 0.3125
- kernel_two: float32 [48, 48, 3, 3], replicated, may hold values from -0.3125 to 0.3125
- moment_one: float32 [48, 48, 3, 3], replicated, may hold values from -6 to 6
- moment_two: float32 [48, 48, 3, 3], replicated, may hold values from -6 to 6
Outputs:
- new_perturb: float32 [48, 64, 2048], P(None, 'rows', 'cols')
- prediction: bfloat16 [48, 32, 1024], P(None, 'rows', 'cols')
- new_kernel_one: float32 [48, 48, 3, 3], replicated
- new_kernel_two: float32 [48, 48, 3, 3], replicated
- new_moment_one: float32 [48, 48, 3, 3], replicated
- new_moment_two: float32 [48, 48, 3, 3], replicated
All inputs are finite; a program needn't handle non-finite values.
Results may differ from a plain program's by a relative error of at most 0.0085.
Values may be sent and summed in bfloat16 or wider, within the bound.
A program may use at most 128 MiB of HBM per device.

v0:
```python
import jax
import jax.numpy as jnp
from jax import lax
from jax.sharding import PartitionSpec as P

REPLAYS = 3
step_size = 0.5
clip_bound = 0.5
momentum_rate = 0.9
learn_rate = 0.005
mean_epsilon = 1e-06
numbers = ("NCHW", "OIHW", "NCHW")


def with_halo(block, sides, width):
    for axis, dim in sides:
        count = lax.axis_size(axis)
        forward = [(i, i + 1) for i in range(count - 1)]
        backward = [(target, source) for source, target in forward]
        low = lax.ppermute(
            lax.slice_in_dim(block, block.shape[dim] - width, None, axis=dim), axis, forward
        )
        high = lax.ppermute(lax.slice_in_dim(block, 0, width, axis=dim), axis, backward)
        block = jnp.concatenate([low, block, high], axis=dim)
    return block


def shifted(block, axis, distance):
    devices = range(lax.axis_size(axis))
    route = [(i - distance, i) for i in devices if i - distance in devices]
    return lax.ppermute(block, axis, route)


def plain_conv(source, kernel, stride, dilation):
    return lax.conv_general_dilated(
        source[None],
        kernel,
        (stride, stride),
        "VALID",
        rhs_dilation=(dilation, dilation),
        dimension_numbers=numbers,
        preferred_element_type=jnp.float32,
    )[0]


def kernel_grad(source, grad_out, stride, dilation):
    summed = lax.conv_general_dilated(
        source[None],
        grad_out[None],
        (dilation, dilation),
        "VALID",
        rhs_dilation=(stride, stride),
        dimension_numbers=("CNHW", "IOHW", "NCHW"),
        preferred_element_type=jnp.float32,
    )
    return jnp.transpose(summed, (1, 0, 2, 3))


def flipped(kernel):
    return jnp.transpose(kernel, (1, 0, 2, 3))[:, :, ::-1, ::-1]


def spread_grad(grad_out, kernel):
    return lax.conv_general_dilated(
        grad_out[None],
        flipped(kernel),
        (1, 1),
        ((2, 2), (2, 2)),
        lhs_dilation=(2, 2),
        dimension_numbers=numbers,
        preferred_element_type=jnp.float32,
    )[0]


def silu_slope(pre_value):
    sigmoid_value = jax.nn.sigmoid(pre_value)
    return sigmoid_value * (1.0 + pre_value * (1.0 - sigmoid_value))


def normed_update(kernel, moment, gradient, mean_square):
    moment = momentum_rate * moment + gradient / jnp.sqrt(mean_square + mean_epsilon)
    return (kernel - learn_rate * moment, moment)


def body(image, perturb, target, kernel_one, kernel_two, moment_one, moment_two):
    target_wide = target.astype(jnp.float32)
    learned = [kernel_one, moment_one, kernel_two, moment_two]
    fast_one = kernel_one.astype(jnp.bfloat16)
    fast_two = kernel_two.astype(jnp.bfloat16)
    predict = jnp.zeros(target.shape, jnp.float32)
    for replay in range(REPLAYS):
        attacked = (image.astype(jnp.float32) + perturb).astype(jnp.bfloat16)
        beside_all = with_halo(attacked, (("rows", 1), ("cols", 2)), 2)
        hidden_pre = plain_conv(beside_all, fast_one, 1, 2)
        hidden = jax.nn.silu(hidden_pre).astype(jnp.bfloat16)
        left_col = shifted(hidden[:, :, -1:], "cols", 1)
        widened = jnp.concatenate([left_col, hidden], axis=2)
        top_row = shifted(widened[:, -1:, :], "rows", 1)
        extended = jnp.concatenate([top_row, widened], axis=1)
        predict = plain_conv(extended, fast_two, 2, 1)
        residual = (predict - target_wide).astype(jnp.bfloat16)
        grad_two = kernel_grad(extended, residual, 2, 1)
        grad_two = lax.psum(grad_two, ("rows", "cols"))
        spread = spread_grad(residual, fast_two)
        from_below = shifted(spread[:, :1, :].astype(jnp.bfloat16), "rows", -1).astype(jnp.float32)
        widened_grad = spread[:, 1:, :].at[:, -1:, :].add(from_below)
        from_right = shifted(widened_grad[:, :, :1], "cols", -1)
        hidden_grad = widened_grad[:, :, 1:].at[:, :, -1:].add(from_right)
        pre_grad = (hidden_grad * silu_slope(hidden_pre)).astype(jnp.bfloat16)
        grad_rimmed = with_halo(pre_grad, (("rows", 1), ("cols", 2)), 2)
        input_grad = plain_conv(grad_rimmed, flipped(fast_one), 1, 2)
        grad_one = kernel_grad(beside_all, pre_grad, 1, 2)
        perturb = jnp.clip(perturb + step_size * jnp.tanh(input_grad), -clip_bound, clip_bound)
        grad_one = lax.psum(grad_one, ("rows", "cols"))
        new_one, new_moment_one = normed_update(
            learned[0], learned[1], grad_one, jnp.mean(grad_one * grad_one)
        )
        new_two, new_moment_two = normed_update(
            learned[2], learned[3], grad_two, jnp.mean(grad_two * grad_two)
        )
        learned = [new_one, new_moment_one, new_two, new_moment_two]
        fast_one = new_one.astype(jnp.bfloat16)
        fast_two = new_two.astype(jnp.bfloat16)
    return (perturb, predict.astype(jnp.bfloat16), learned[0], learned[2], learned[1], learned[3])


def solution(mesh):
    in_specs = (
        P(None, "rows", "cols"),
        P(None, "rows", "cols"),
        P(None, "rows", "cols"),
        P(),
        P(),
        P(),
        P(),
    )
    out_specs = (P(None, "rows", "cols"), P(None, "rows", "cols"), P(), P(), P(), P())
    return jax.shard_map(body, mesh=mesh, in_specs=in_specs, out_specs=out_specs, check_vma=False)
```

profile of v0, /device:TPU:8, one launch (start us, length us, event | category | flops | bytes accessed | tf_op | source)
XLA Modules:
  0.0 782.5 jit_solution(5333286303783374361)
XLA Ops:
  28.6 7.8 collective-permute-done.3
  80.5 5.1 scatter-add.20
  93.5 4.9 copy.320
  98.4 4.7 copy.329
  106.5 5.5 collective-permute-start.8
  113.3 5.5 fusion.109
  127.2 14.8 %fusion.22 = f32[48,48,3,3]{0,1,3,2:T(8,128)} fusion(bf16[1,48,20,260]{1,0,3,2:T(2,128)(2,1)} %copy.320, bf16[1,48,16,256]{1,2,3,0:T(8,128)(2,1)S(1)} %bitcast.267), kind=kOutput, calls=%fused_computation.48 | convolution fusion | flops 169869312 | bytes 975360 | tf_op jit(solution)/shard_map/transpose | solution.py:56
  158.1 113.7 %all-reduce.11.cloned.1.call-done = (f32[48,48,3,3]{0,1,3,2:T(8,128)}, f32[48,48,3,3]{0,1,3,2:T(8,128)}) async-done(((f32[48,48,3,3]{0,1,3,2:T(8,128)}, f32[48,48,3,3]{0,1,3,2:T(8,128)}), (f32[48,48,3,3]{0,1,3,2:T(8,128)}, f32[48,48,3,3]{0,1,3,2:T(8,128)})) %all-reduce.11.cloned.1.call-update) | async-done | bytes 165904 | tf_op jit(solution)/shard_map/psum | solution.py:114
  282.9 4.1 collective-permute-done.14
  329.9 5.1 scatter-add.24
  337.6 4.9 copy.348
  342.5 4.7 copy.355
  350.6 6.2 collective-permute-start.20
  358.1 5.5 fusion.107
  371.8 14.8 %fusion.20 = f32[48,48,3,3]{0,1,3,2:T(8,128)} fusion(bf16[1,48,20,260]{1,0,3,2:T(2,128)(2,1)} %copy.348, bf16[1,48,16,256]{1,2,3,0:T(8,128)(2,1)S(1)} %bitcast.268), kind=kOutput, calls=%fused_computation.46 | convolution fusion | flops 169869312 | bytes 975360 | tf_op jit(solution)/shard_map/transpose | solution.py:56
  403.4 112.0 %all-reduce.9.cloned.1.call-done = (f32[48,48,3,3]{0,1,3,2:T(8,128)}, f32[48,48,3,3]{0,1,3,2:T(8,128)}) async-done(((f32[48,48,3,3]{0,1,3,2:T(8,128)}, f32[48,48,3,3]{0,1,3,2:T(8,128)}), (f32[48,48,3,3]{0,1,3,2:T(8,128)}, f32[48,48,3,3]{0,1,3,2:T(8,128)})) %all-reduce.9.cloned.1.call-update) | async-done | bytes 165904 | tf_op jit(solution)/shard_map/psum | solution.py:114
  527.4 4.2 collective-permute-done.26
  574.5 4.9 copy.368
  582.9 4.7 copy.370
  589.0 5.1 scatter-add.26
  596.7 7.1 fusion.105
  605.0 4.8 collective-permute-start.32
  622.2 14.8 %fusion.18 = f32[48,48,3,3]{0,1,3,2:T(8,128)} fusion(bf16[1,48,20,260]{1,0,3,2:T(2,128)(2,1)} %copy.368, bf16[1,48,16,256]{1,2,3,0:T(8,128)(2,1)S(1)} %bitcast.269), kind=kOutput, calls=%fused_computation.44 | convolution fusion | flops 169869312 | bytes 975360 | tf_op jit(solution)/shard_map/transpose | solution.py:56
  650.2 117.2 %all-reduce.7.cloned.1.call-done = (f32[48,48,3,3]{0,1,3,2:T(8,128)}, f32[48,48,3,3]{0,1,3,2:T(8,128)}) async-done(((f32[48,48,3,3]{0,1,3,2:T(8,128)}, f32[48,48,3,3]{0,1,3,2:T(8,128)}), (f32[48,48,3,3]{0,1,3,2:T(8,128)}, f32[48,48,3,3]{0,1,3,2:T(8,128)})) %all-reduce.7.cloned.1.call-update) | async-done | bytes 165904 | tf_op jit(solution)/shard_map/psum | solution.py:114
  (396 shorter events, 280.0 us)
Async XLA Ops:
  7.2 264.7 %all-reduce.11.cloned.1.call-start = ((), (), s32[]{:S(2)}) async-start(), calls=%async_computation.2 | async-start | bytes 884736 | tf_op jit(solution)/shard_map/psum | solution.py:114
  23.0 13.4 %collective-permute-start.3 = (bf16[48,20,2]{2,0,1:T(8,128)(2,1)S(1)}, bf16[48,20,2]{2,0,1:T(8,128)(2,1)S(1)}, u32[]{:S(2)}, u32[]{:S(2)}) collective-permute-start(bf16[48,20,2]{2,0,1:T(8,128)(2,1)S(1)} %get-tuple-element.163), channel_id=1, source_target_pairs={{1,0},{2,1},{3,2},{4,3},{5,4},{6,5},{7,6},{9,8},{10,9},{11,10},{12... | collective-permute-start | bytes 11528 | tf_op jit(solution)/shard_map/ppermute | solution.py:23
  86.3 18.5 %collective-permute-start.7 = (f32[48,16,1]{0,1,2:T(8,128)S(1)}, f32[48,16,1]{0,1,2:T(8,128)S(1)}, u32[]{:S(2)}, u32[]{:S(2)}) collective-permute-start(f32[48,16,1]{0,1,2:T(8,128)S(1)} %slice.369), channel_id=1, source_target_pairs={{1,0},{2,1},{3,2},{4,3},{5,4},{6,5},{7,6},{9,8},{10,9},{11,10},{12... | collective-permute-start | bytes 9224 | tf_op jit(solution)/shard_map/ppermute | solution.py:31
  106.5 13.2 %collective-permute-start.8 = (bf16[48,2,256]{0,1,2:T(2,128)(2,1)S(1)}, bf16[48,2,256]{0,1,2:T(2,128)(2,1)S(1)}, u32[]{:S(2)}, u32[]{:S(2)}) collective-permute-start(bf16[48,2,256]{0,1,2:T(2,128)(2,1)S(1)} %get-tuple-element.130), channel_id=1, source_target_pairs={{0,8},{8,16},{16,24},{1,9},{9,17},{17,25},{2,10},{10,18},{18,26},{... | collective-permute-start | bytes 147464 | tf_op jit(solution)/shard_map/ppermute | solution.py:20
  120.1 22.2 %collective-permute-start.10 = (bf16[48,20,2]{2,0,1:T(8,128)(2,1)S(1)}, bf16[48,20,2]{2,0,1:T(8,128)(2,1)S(1)}, u32[]{:S(2)}, u32[]{:S(2)}) collective-permute-start(bf16[48,20,2]{2,0,1:T(8,128)(2,1)S(1)} %get-tuple-element.160), channel_id=1, source_target_pairs={{0,1},{1,2},{2,3},{3,4},{4,5},{5,6},{6,7},{8,9},{9,10},{10,11},{11... | collective-permute-start | bytes 11528 | tf_op jit(solution)/shard_map/ppermute | solution.py:20
  123.7 18.5 %collective-permute-start.11 = (bf16[48,20,2]{2,0,1:T(8,128)(2,1)S(1)}, bf16[48,20,2]{2,0,1:T(8,128)(2,1)S(1)}, u32[]{:S(2)}, u32[]{:S(2)}) collective-permute-start(bf16[48,20,2]{2,0,1:T(8,128)(2,1)S(1)} %get-tuple-element.161), channel_id=1, source_target_pairs={{1,0},{2,1},{3,2},{4,3},{5,4},{6,5},{7,6},{9,8},{10,9},{11,10},{12... | collective-permute-start | bytes 11528 | tf_op jit(solution)/shard_map/ppermute | solution.py:23
  142.0 373.5 %all-reduce.9.cloned.1.call-start = ((), (), s32[]{:S(2)}) async-start(), calls=%async_computation.1 | async-start | bytes 884736 | tf_op jit(solution)/shard_map/psum | solution.py:114
  154.3 120.0 %collective-permute-start.12 = (bf16[48,2,256]{0,1,2:T(2,128)(2,1)S(1)}, bf16[48,2,256]{0,1,2:T(2,128)(2,1)S(1)}, u32[]{:S(2)}, u32[]{:S(2)}) collective-permute-start(bf16[48,2,256]{0,1,2:T(2,128)(2,1)S(1)} %get-tuple-element.128), channel_id=1, source_target_pairs={{0,8},{8,16},{16,24},{1,9},{9,17},{17,25},{2,10},{10,18},{18,26},{... | collective-permute-start | bytes 147464 | tf_op jit(solution)/shard_map/ppermute | solution.py:20
  156.8 117.6 %collective-permute-start.13 = (bf16[48,2,256]{0,1,2:T(2,128)(2,1)S(1)}, bf16[48,2,256]{0,1,2:T(2,128)(2,1)S(1)}, u32[]{:S(2)}, u32[]{:S(2)}) collective-permute-start(bf16[48,2,256]{0,1,2:T(2,128)(2,1)S(1)} %get-tuple-element.129), channel_id=1, source_target_pairs={{8,0},{16,8},{24,16},{9,1},{17,9},{25,17},{10,2},{18,10},{26,18},{... | collective-permute-start | bytes 147464 | tf_op jit(solution)/shard_map/ppermute | solution.py:23
  274.7 12.3 %collective-permute-start.14 = (bf16[48,20,2]{2,0,1:T(8,128)(2,1)S(1)}, bf16[48,20,2]{2,0,1:T(8,128)(2,1)S(1)}, u32[]{:S(2)}, u32[]{:S(2)}) collective-permute-start(bf16[48,20,2]{2,0,1:T(8,128)(2,1)S(1)} %get-tuple-element.158), channel_id=1, source_target_pairs={{0,1},{1,2},{2,3},{3,4},{4,5},{5,6},{6,7},{8,9},{9,10},{10,11},{11... | collective-permute-start | bytes 11528 | tf_op jit(solution)/shard_map/ppermute | solution.py:20
  278.1 10.6 %collective-permute-start.15 = (bf16[48,20,2]{2,0,1:T(8,128)(2,1)S(1)}, bf16[48,20,2]{2,0,1:T(8,128)(2,1)S(1)}, u32[]{:S(2)}, u32[]{:S(2)}) collective-permute-start(bf16[48,20,2]{2,0,1:T(8,128)(2,1)S(1)} %get-tuple-element.159), channel_id=1, source_target_pairs={{1,0},{2,1},{3,2},{4,3},{5,4},{6,5},{7,6},{9,8},{10,9},{11,10},{12... | collective-permute-start | bytes 11528 | tf_op jit(solution)/shard_map/ppermute | solution.py:23
  335.6 13.3 %collective-permute-start.19 = (f32[48,16,1]{0,1,2:T(8,128)S(1)}, f32[48,16,1]{0,1,2:T(8,128)S(1)}, u32[]{:S(2)}, u32[]{:S(2)}) collective-permute-start(f32[48,16,1]{0,1,2:T(8,128)S(1)} %slice.394), channel_id=1, source_target_pairs={{1,0},{2,1},{3,2},{4,3},{5,4},{6,5},{7,6},{9,8},{10,9},{11,10},{12... | collective-permute-start | bytes 9224 | tf_op jit(solution)/shard_map/ppermute | solution.py:31
  350.6 13.9 %collective-permute-start.20 = (bf16[48,2,256]{0,1,2:T(2,128)(2,1)S(1)}, bf16[48,2,256]{0,1,2:T(2,128)(2,1)S(1)}, u32[]{:S(2)}, u32[]{:S(2)}) collective-permute-start(bf16[48,2,256]{0,1,2:T(2,128)(2,1)S(1)} %get-tuple-element.126), channel_id=1, source_target_pairs={{0,8},{8,16},{16,24},{1,9},{9,17},{17,25},{2,10},{10,18},{18,26},{... | collective-permute-start | bytes 147464 | tf_op jit(solution)/shard_map/ppermute | solution.py:20
  364.9 22.2 %collective-permute-start.22 = (bf16[48,20,2]{2,0,1:T(8,128)(2,1)S(1)}, bf16[48,20,2]{2,0,1:T(8,128)(2,1)S(1)}, u32[]{:S(2)}, u32[]{:S(2)}) collective-permute-start(bf16[48,20,2]{2,0,1:T(8,128)(2,1)S(1)} %get-tuple-element.156), channel_id=1, source_target_pairs={{0,1},{1,2},{2,3},{3,4},{4,5},{5,6},{6,7},{8,9},{9,10},{10,11},{11... | collective-permute-start | bytes 11528 | tf_op jit(solution)/shard_map/ppermute | solution.py:20
  368.5 18.5 %collective-permute-start.23 = (bf16[48,20,2]{2,0,1:T(8,128)(2,1)S(1)}, bf16[48,20,2]{2,0,1:T(8,128)(2,1)S(1)}, u32[]{:S(2)}, u32[]{:S(2)}) collective-permute-start(bf16[48,20,2]{2,0,1:T(8,128)(2,1)S(1)} %get-tuple-element.157), channel_id=1, source_target_pairs={{1,0},{2,1},{3,2},{4,3},{5,4},{6,5},{7,6},{9,8},{10,9},{11,10},{12... | collective-permute-start | bytes 11528 | tf_op jit(solution)/shard_map/ppermute | solution.py:23
  386.6 380.8 %all-reduce.7.cloned.1.call-start = ((), (), s32[]{:S(2)}) async-start(), calls=%async_computation | async-start | bytes 884736 | tf_op jit(solution)/shard_map/psum | solution.py:114
  399.6 119.2 %collective-permute-start.24 = (bf16[48,2,256]{0,1,2:T(2,128)(2,1)S(1)}, bf16[48,2,256]{0,1,2:T(2,128)(2,1)S(1)}, u32[]{:S(2)}, u32[]{:S(2)}) collective-permute-start(bf16[48,2,256]{0,1,2:T(2,128)(2,1)S(1)} %get-tuple-element.124), channel_id=1, source_target_pairs={{0,8},{8,16},{16,24},{1,9},{9,17},{17,25},{2,10},{10,18},{18,26},{... | collective-permute-start | bytes 147464 | tf_op jit(solution)/shard_map/ppermute | solution.py:20
  402.1 116.8 %collective-permute-start.25 = (bf16[48,2,256]{0,1,2:T(2,128)(2,1)S(1)}, bf16[48,2,256]{0,1,2:T(2,128)(2,1)S(1)}, u32[]{:S(2)}, u32[]{:S(2)}) collective-permute-start(bf16[48,2,256]{0,1,2:T(2,128)(2,1)S(1)} %get-tuple-element.125), channel_id=1, source_target_pairs={{8,0},{16,8},{24,16},{9,1},{17,9},{25,17},{10,2},{18,10},{26,18},{... | collective-permute-start | bytes 147464 | tf_op jit(solution)/shard_map/ppermute | solution.py:23
  519.3 12.3 %collective-permute-start.26 = (bf16[48,20,2]{2,0,1:T(8,128)(2,1)S(1)}, bf16[48,20,2]{2,0,1:T(8,128)(2,1)S(1)}, u32[]{:S(2)}, u32[]{:S(2)}) collective-permute-start(bf16[48,20,2]{2,0,1:T(8,128)(2,1)S(1)} %get-tuple-element.154), channel_id=1, source_target_pairs={{0,1},{1,2},{2,3},{3,4},{4,5},{5,6},{6,7},{8,9},{9,10},{10,11},{11... | collective-permute-start | bytes 11528 | tf_op jit(solution)/shard_map/ppermute | solution.py:20
  522.6 10.6 %collective-permute-start.27 = (bf16[48,20,2]{2,0,1:T(8,128)(2,1)S(1)}, bf16[48,20,2]{2,0,1:T(8,128)(2,1)S(1)}, u32[]{:S(2)}, u32[]{:S(2)}) collective-permute-start(bf16[48,20,2]{2,0,1:T(8,128)(2,1)S(1)} %get-tuple-element.155), channel_id=1, source_target_pairs={{1,0},{2,1},{3,2},{4,3},{5,4},{6,5},{7,6},{9,8},{10,9},{11,10},{12... | collective-permute-start | bytes 11528 | tf_op jit(solution)/shard_map/ppermute | solution.py:23
  573.2 14.4 %collective-permute-start.30 = (bf16[48,1,257]{0,1,2:T(2,128)(2,1)}, bf16[48,1,257]{0,1,2:T(2,128)(2,1)}, u32[]{:S(2)}, u32[]{:S(2)}) collective-permute-start(bf16[48,1,257]{0,1,2:T(2,128)(2,1)} %slice.527), channel_id=1, source_target_pairs={{8,0},{16,8},{24,16},{9,1},{17,9},{25,17},{10,2},{18,10},{26,18},{... | collective-permute-start | bytes 74024 | tf_op jit(solution)/shard_map/ppermute | solution.py:31
  594.8 9.2 %collective-permute-start.31 = (f32[48,16,1]{0,1,2:T(8,128)S(1)}, f32[48,16,1]{0,1,2:T(8,128)S(1)}, u32[]{:S(2)}, u32[]{:S(2)}) collective-permute-start(f32[48,16,1]{0,1,2:T(8,128)S(1)} %slice.419), channel_id=1, source_target_pairs={{1,0},{2,1},{3,2},{4,3},{5,4},{6,5},{7,6},{9,8},{10,9},{11,10},{12... | collective-permute-start | bytes 9224 | tf_op jit(solution)/shard_map/ppermute | solution.py:31
  615.3 21.8 %collective-permute-start.34 = (bf16[48,20,2]{2,0,1:T(8,128)(2,1)S(1)}, bf16[48,20,2]{2,0,1:T(8,128)(2,1)S(1)}, u32[]{:S(2)}, u32[]{:S(2)}) collective-permute-start(bf16[48,20,2]{2,0,1:T(8,128)(2,1)S(1)} %get-tuple-element.152), channel_id=1, source_target_pairs={{0,1},{1,2},{2,3},{3,4},{4,5},{5,6},{6,7},{8,9},{9,10},{10,11},{11... | collective-permute-start | bytes 11528 | tf_op jit(solution)/shard_map/ppermute | solution.py:20
  619.2 17.8 %collective-permute-start.35 = (bf16[48,20,2]{2,0,1:T(8,128)(2,1)S(1)}, bf16[48,20,2]{2,0,1:T(8,128)(2,1)S(1)}, u32[]{:S(2)}, u32[]{:S(2)}) collective-permute-start(bf16[48,20,2]{2,0,1:T(8,128)(2,1)S(1)} %get-tuple-element.153), channel_id=1, source_target_pairs={{1,0},{2,1},{3,2},{4,3},{5,4},{6,5},{7,6},{9,8},{10,9},{11,10},{12... | collective-permute-start | bytes 11528 | tf_op jit(solution)/shard_map/ppermute | solution.py:23
  (83 other events, 1533.5 us)
Sparse Core Ops, SparseCore 0:
  142.1 129.6 all-reduce.10
  386.7 128.7 all-reduce.8
  637.1 130.2 all-reduce.6
where the time goes:
time: 792 us; the launch traced here: 782 us
  waiting for transfers between devices  378 us (48%)
  local copies, waits for them, and re-layouts  163 us (21%)
  starting transfers between devices  95.5 us (12%)
  matrix products  89.8 us (11%)
  other arithmetic  35.4 us (4%)
  between operations  20.5 us (3%)
    psum x3, waiting for transfers between devices, body(): grad_one = lax.psum(grad_one, ('rows', 'cols'))  343 us
    transpose x6, matrix products, kernel_grad(): return jnp.transpose(summed, (1, 0, 2, 3))  62.4 us
    conv_general_dilated x33, local copies, waits for them, and re-layouts, plain_conv(): lax.conv_general_dilated(source[None], kernel, (stride, stride), 'VALID',...  54.5 us
    ppermute x12, starting transfers between devices, with_halo(): lax.ppermute(lax.slice_in_dim(block, block.shape[dim] - width, None, axis...  44.4 us
    broadcast_in_dim x15, local copies, waits for them, and re-layouts, plain_conv(): source[None]  32 us
    ppermute x12, starting transfers between devices, with_halo(): lax.ppermute(lax.slice_in_dim(block, 0, width, axis=dim), axis, backward)  27.7 us
    unnamed x149, local copies, waits for them, and re-layouts  26.4 us
    conv_general_dilated x9, matrix products, plain_conv(): lax.conv_general_dilated(source[None], kernel, (stride, stride), 'VALID',...  23.4 us
  transfers between devices with their start and end apart: 39, of which 16 were waited for; matrix products, arithmetic and copies ran while one was open for 20% of the time, Pallas kernels for 0%

commit v1 on v0

--- a/solution.py
+++ b/solution.py
@@ -111,7 +111,7 @@
         input_grad = plain_conv(grad_rimmed, flipped(fast_one), 1, 2)
         grad_one = kernel_grad(beside_all, pre_grad, 1, 2)
         perturb = jnp.clip(perturb + step_size * jnp.tanh(input_grad), -clip_bound, clip_bound)
-        grad_one = lax.psum(grad_one, ("rows", "cols"))
+        grad_one = lax.psum(lax.psum(grad_one, "cols"), "rows")
         new_one, new_moment_one = normed_update(
             learned[0], learned[1], grad_one, jnp.mean(grad_one * grad_one)
         )

time: 792 us -> 1040 us (1.31)
  waiting for transfers between devices: 378 us -> 569 us
  local copies, waits for them, and re-layouts: 163 us -> 199 us
  other arithmetic: 35.4 us -> 50.4 us
    psum x3 -> x9, waiting for transfers between devices: 343 us -> 534 us  [the longest x6 269 us: body(): grad_one = lax.psum(lax.psum(grad_one, 'cols'), 'rows')]
    broadcast_in_dim x15, local copies, waits for them, and re-layouts: 32 us -> 42.7 us  [plain_conv(): source[None]]
    unnamed x149 -> x135, local copies, waits for them, and re-layouts: 26.4 us -> 30.3 us
  transfers between devices with their start and end apart: 39 -> 45, of which waited for: 16 -> 22; matrix products, arithmetic and copies ran while one was open for 20% -> 20% of each run, Pallas kernels for 0% -> 0%
where the time goes in v1:
time: 1040 us; the launch traced here: 1030 us
  waiting for transfers between devices  569 us (55%)
  local copies, waits for them, and re-layouts  199 us (19%)
  starting transfers between devices  96.4 us (9%)
  matrix products  91.1 us (9%)
  other arithmetic  50.4 us (5%)
  between operations  20.1 us (2%)
    psum x6, waiting for transfers between devices, body(): grad_one = lax.psum(lax.psum(grad_one, 'cols'), 'rows')  269 us
    psum x3, waiting for transfers between devices, body(): grad_two = lax.psum(grad_two, ('rows', 'cols'))  265 us
    conv_general_dilated x33, local copies, waits for them, and re-layouts, plain_conv(): lax.conv_general_dilated(source[None], kernel, (stride, stride), 'VALID',...  63.2 us
    transpose x6, matrix products, kernel_grad(): return jnp.transpose(summed, (1, 0, 2, 3))  60 us
    broadcast_in_dim x15, local copies, waits for them, and re-layouts, plain_conv(): source[None]  42.7 us
    ppermute x12, starting transfers between devices, with_halo(): lax.ppermute(lax.slice_in_dim(block, block.shape[dim] - width, None, axis...  37.9 us
    ppermute x12, starting transfers between devices, with_halo(): lax.ppermute(lax.slice_in_dim(block, 0, width, axis=dim), axis, backward)  31.8 us
    unnamed x135, local copies, waits for them, and re-layouts  30.3 us
  transfers between devices with their start and end apart: 45, of which 22 were waited for; matrix products, arithmetic and copies ran while one was open for 20% of the time, Pallas kernels for 0%

profile of v1, /device:TPU:8, one launch (start us, length us, event | category | flops | bytes accessed | tf_op | source)
XLA Modules:
  0.0 1026.1 jit_solution(16068005746018079616)
XLA Ops:
  33.0 7.0 collective-permute-done.3
  96.8 5.1 scatter-add.20
  123.9 7.3 copy.320
  131.2 6.5 copy.329
  151.6 6.9 fusion.109
  183.9 13.0 %fusion.22 = f32[48,48,3,3]{0,1,3,2:T(8,128)} fusion(bf16[1,48,20,260]{1,0,3,2:T(2,128)(2,1)S(1)} %copy-done.21, bf16[1,48,16,256]{1,2,3,0:T(8,128)(2,1)S(1)} %bitcast.267), kind=kOutput, calls=%fused_computation.48 | convolution fusion | flops 169869312 | bytes 975360 | tf_op jit(solution)/shard_map/transpose | solution.py:56
  205.0 80.1 %all-reduce.14.cloned.1.call-done = f32[48,48,3,3]{0,1,3,2:T(8,128)} async-done(((f32[48,48,3,3]{0,1,3,2:T(8,128)}), f32[48,48,3,3]{0,1,3,2:T(8,128)}) %all-reduce.14.cloned.1.call-update) | async-done | bytes 82960 | tf_op jit(solution)/shard_map/psum | solution.py:103
  287.3 70.6 %all-reduce.10.cloned.1.call-done = f32[48,48,3,3]{0,1,3,2:T(8,128)} async-done(((f32[48,48,3,3]{0,1,3,2:T(8,128)}), f32[48,48,3,3]{0,1,3,2:T(8,128)}) %all-reduce.10.cloned.1.call-update) | async-done | bytes 82960 | tf_op jit(solution)/shard_map/psum | solution.py:114
  364.7 27.2 %all-reduce.12.cloned.1.call-done = f32[48,48,3,3]{0,1,3,2:T(8,128)} async-done(((f32[48,48,3,3]{0,1,3,2:T(8,128)}), f32[48,48,3,3]{0,1,3,2:T(8,128)}) %all-reduce.12.cloned.1.call-update) | async-done | bytes 82960 | tf_op jit(solution)/shard_map/psum | solution.py:114
  426.6 5.1 scatter-add.24
  439.6 5.0 collective-permute-start.20
  446.0 7.3 copy.348
  466.0 6.8 fusion.107
  496.2 13.0 %fusion.20 = f32[48,48,3,3]{0,1,3,2:T(8,128)} fusion(bf16[1,48,20,260]{1,0,3,2:T(2,128)(2,1)S(1)} %copy-done.20, bf16[1,48,16,256]{1,2,3,0:T(8,128)(2,1)S(1)} %bitcast.268), kind=kOutput, calls=%fused_computation.46 | convolution fusion | flops 169869312 | bytes 975360 | tf_op jit(solution)/shard_map/transpose | solution.py:56
  517.3 82.6 %all-reduce.20.cloned.1.call-done = f32[48,48,3,3]{0,1,3,2:T(8,128)} async-done(((f32[48,48,3,3]{0,1,3,2:T(8,128)}), f32[48,48,3,3]{0,1,3,2:T(8,128)}) %all-reduce.20.cloned.1.call-update) | async-done | bytes 82960 | tf_op jit(solution)/shard_map/psum | solution.py:103
  602.2 70.4 %all-reduce.16.cloned.1.call-done = f32[48,48,3,3]{0,1,3,2:T(8,128)} async-done(((f32[48,48,3,3]{0,1,3,2:T(8,128)}), f32[48,48,3,3]{0,1,3,2:T(8,128)}) %all-reduce.16.cloned.1.call-update) | async-done | bytes 82960 | tf_op jit(solution)/shard_map/psum | solution.py:114
  680.0 26.4 %all-reduce.18.cloned.1.call-done = f32[48,48,3,3]{0,1,3,2:T(8,128)} async-done(((f32[48,48,3,3]{0,1,3,2:T(8,128)}), f32[48,48,3,3]{0,1,3,2:T(8,128)}) %all-reduce.18.cloned.1.call-update) | async-done | bytes 82960 | tf_op jit(solution)/shard_map/psum | solution.py:114
  719.5 7.3 copy.368
  757.6 5.5 fusion.105
  768.0 5.1 scatter-add.26
  787.8 14.8 %fusion.18 = f32[48,48,3,3]{0,1,3,2:T(8,128)} fusion(bf16[1,48,20,260]{1,0,3,2:T(2,128)(2,1)} %copy.368, bf16[1,48,16,256]{1,2,3,0:T(8,128)(2,1)S(1)} %bitcast.269), kind=kOutput, calls=%fused_computation.44 | convolution fusion | flops 169869312 | bytes 975360 | tf_op jit(solution)/shard_map/transpose | solution.py:56
  802.6 101.8 %all-reduce.26.cloned.1.call-done = f32[48,48,3,3]{0,1,3,2:T(8,128)} async-done(((f32[48,48,3,3]{0,1,3,2:T(8,128)}), f32[48,48,3,3]{0,1,3,2:T(8,128)}) %all-reduce.26.cloned.1.call-update) | async-done | bytes 82960 | tf_op jit(solution)/shard_map/psum | solution.py:103
  931.5 48.9 %all-reduce.22.cloned.1.call-done = f32[48,48,3,3]{0,1,3,2:T(8,128)} async-done(((f32[48,48,3,3]{0,1,3,2:T(8,128)}), f32[48,48,3,3]{0,1,3,2:T(8,128)}) %all-reduce.22.cloned.1.call-update) | async-done | bytes 82960 | tf_op jit(solution)/shard_map/psum | solution.py:114
  988.8 25.6 %all-reduce.24.cloned.1.call-done = f32[48,48,3,3]{0,1,3,2:T(8,128)} async-done(((f32[48,48,3,3]{0,1,3,2:T(8,128)}), f32[48,48,3,3]{0,1,3,2:T(8,128)}) %all-reduce.24.cloned.1.call-update) | async-done | bytes 82960 | tf_op jit(solution)/shard_map/psum | solution.py:114
  (401 shorter events, 356.8 us)
Async XLA Ops:
  7.2 277.9 %all-reduce.14.cloned.1.call-start = ((), (), s32[]{:S(2)}) async-start(), calls=%async_computation.2 | async-start | bytes 442368 | tf_op jit(solution)/shard_map/psum | solution.py:103
  111.6 28.1 %collective-permute-start.8 = (bf16[48,2,256]{0,1,2:T(2,128)(2,1)}, bf16[48,2,256]{0,1,2:T(2,128)(2,1)}, u32[]{:S(2)}, u32[]{:S(2)}) collective-permute-start(bf16[48,2,256]{0,1,2:T(2,128)(2,1)} %get-tuple-element.124), channel_id=1, source_target_pairs={{0,8},{8,16},{16,24},{1,9},{9,17},{17,25},{2,10},{10,18},{18,26},{... | collective-permute-start | bytes 147464 | tf_op jit(solution)/shard_map/ppermute | solution.py:20
  116.6 24.7 %collective-permute-start.9 = (bf16[48,2,256]{0,1,2:T(2,128)(2,1)}, bf16[48,2,256]{0,1,2:T(2,128)(2,1)}, u32[]{:S(2)}, u32[]{:S(2)}) collective-permute-start(bf16[48,2,256]{0,1,2:T(2,128)(2,1)} %get-tuple-element.125), channel_id=1, source_target_pairs={{8,0},{16,8},{24,16},{9,1},{17,9},{25,17},{10,2},{18,10},{26,18},{... | collective-permute-start | bytes 147464 | tf_op jit(solution)/shard_map/ppermute | solution.py:23
  144.7 14.8 %collective-permute-start.10 = (bf16[48,20,2]{2,0,1:T(8,128)(2,1)}, bf16[48,20,2]{2,0,1:T(8,128)(2,1)}, u32[]{:S(2)}, u32[]{:S(2)}) collective-permute-start(bf16[48,20,2]{2,0,1:T(8,128)(2,1)} %get-tuple-element.154), channel_id=1, source_target_pairs={{0,1},{1,2},{2,3},{3,4},{4,5},{5,6},{6,7},{8,9},{9,10},{10,11},{11... | collective-permute-start | bytes 11528 | tf_op jit(solution)/shard_map/ppermute | solution.py:20
  158.5 199.4 %all-reduce.10.cloned.1.call-start = ((), (), s32[]{:S(2)}) async-start(), calls=%async_computation | async-start | bytes 442368 | tf_op jit(solution)/shard_map/psum | solution.py:114
  180.3 17.5 %collective-permute-start.12 = (bf16[48,2,256]{0,1,2:T(2,128)(2,1)S(1)}, bf16[48,2,256]{0,1,2:T(2,128)(2,1)S(1)}, u32[]{:S(2)}, u32[]{:S(2)}) collective-permute-start(bf16[48,2,256]{0,1,2:T(2,128)(2,1)S(1)} %get-tuple-element.122), channel_id=1, source_target_pairs={{0,8},{8,16},{16,24},{1,9},{9,17},{17,25},{2,10},{10,18},{18,26},{... | collective-permute-start | bytes 147464 | tf_op jit(solution)/shard_map/ppermute | solution.py:20
  182.3 15.6 %collective-permute-start.13 = (bf16[48,2,256]{0,1,2:T(2,128)(2,1)S(1)}, bf16[48,2,256]{0,1,2:T(2,128)(2,1)S(1)}, u32[]{:S(2)}, u32[]{:S(2)}) collective-permute-start(bf16[48,2,256]{0,1,2:T(2,128)(2,1)S(1)} %get-tuple-element.123), channel_id=1, source_target_pairs={{8,0},{16,8},{24,16},{9,1},{17,9},{25,17},{10,2},{18,10},{26,18},{... | collective-permute-start | bytes 147464 | tf_op jit(solution)/shard_map/ppermute | solution.py:23
  196.9 195.0 %all-reduce.12.cloned.1.call-start = ((), (), s32[]{:S(2)}) async-start(), calls=%async_computation.1 | async-start | bytes 442368 | tf_op jit(solution)/shard_map/psum | solution.py:114
  198.2 160.2 %collective-permute-start.14 = (bf16[48,20,2]{2,0,1:T(8,128)(2,1)S(1)}, bf16[48,20,2]{2,0,1:T(8,128)(2,1)S(1)}, u32[]{:S(2)}, u32[]{:S(2)}) collective-permute-start(bf16[48,20,2]{2,0,1:T(8,128)(2,1)S(1)} %get-tuple-element.152), channel_id=1, source_target_pairs={{0,1},{1,2},{2,3},{3,4},{4,5},{5,6},{6,7},{8,9},{9,10},{10,11},{11... | collective-permute-start | bytes 11528 | tf_op jit(solution)/shard_map/ppermute | solution.py:20
  200.4 158.1 %collective-permute-start.15 = (bf16[48,20,2]{2,0,1:T(8,128)(2,1)S(1)}, bf16[48,20,2]{2,0,1:T(8,128)(2,1)S(1)}, u32[]{:S(2)}, u32[]{:S(2)}) collective-permute-start(bf16[48,20,2]{2,0,1:T(8,128)(2,1)S(1)} %get-tuple-element.153), channel_id=1, source_target_pairs={{1,0},{2,1},{3,2},{4,3},{5,4},{6,5},{7,6},{9,8},{10,9},{11,10},{12... | collective-permute-start | bytes 11528 | tf_op jit(solution)/shard_map/ppermute | solution.py:23
  357.9 242.0 %all-reduce.20.cloned.1.call-start = ((), (), s32[]{:S(2)}) async-start(), calls=%async_computation.5 | async-start | bytes 442368 | tf_op jit(solution)/shard_map/psum | solution.py:103
  439.6 19.2 %collective-permute-start.20 = (bf16[48,2,256]{0,1,2:T(2,128)(2,1)S(1)}, bf16[48,2,256]{0,1,2:T(2,128)(2,1)S(1)}, u32[]{:S(2)}, u32[]{:S(2)}) collective-permute-start(bf16[48,2,256]{0,1,2:T(2,128)(2,1)S(1)} %get-tuple-element.120), channel_id=1, source_target_pairs={{0,8},{8,16},{16,24},{1,9},{9,17},{17,25},{2,10},{10,18},{18,26},{... | collective-permute-start | bytes 147464 | tf_op jit(solution)/shard_map/ppermute | solution.py:20
  444.7 14.2 %collective-permute-start.21 = (bf16[48,2,256]{0,1,2:T(2,128)(2,1)S(1)}, bf16[48,2,256]{0,1,2:T(2,128)(2,1)S(1)}, u32[]{:S(2)}, u32[]{:S(2)}) collective-permute-start(bf16[48,2,256]{0,1,2:T(2,128)(2,1)S(1)} %get-tuple-element.121), channel_id=1, source_target_pairs={{8,0},{16,8},{24,16},{9,1},{17,9},{25,17},{10,2},{18,10},{26,18},{... | collective-permute-start | bytes 147464 | tf_op jit(solution)/shard_map/ppermute | solution.py:23
  472.8 199.8 %all-reduce.16.cloned.1.call-start = ((), (), s32[]{:S(2)}) async-start(), calls=%async_computation.3 | async-start | bytes 442368 | tf_op jit(solution)/shard_map/psum | solution.py:114
  492.3 17.8 %collective-permute-start.24 = (bf16[48,2,256]{0,1,2:T(2,128)(2,1)S(1)}, bf16[48,2,256]{0,1,2:T(2,128)(2,1)S(1)}, u32[]{:S(2)}, u32[]{:S(2)}) collective-permute-start(bf16[48,2,256]{0,1,2:T(2,128)(2,1)S(1)} %get-tuple-element.118), channel_id=1, source_target_pairs={{0,8},{8,16},{16,24},{1,9},{9,17},{17,25},{2,10},{10,18},{18,26},{... | collective-permute-start | bytes 147464 | tf_op jit(solution)/shard_map/ppermute | solution.py:20
  494.5 15.7 %collective-permute-start.25 = (bf16[48,2,256]{0,1,2:T(2,128)(2,1)S(1)}, bf16[48,2,256]{0,1,2:T(2,128)(2,1)S(1)}, u32[]{:S(2)}, u32[]{:S(2)}) collective-permute-start(bf16[48,2,256]{0,1,2:T(2,128)(2,1)S(1)} %get-tuple-element.119), channel_id=1, source_target_pairs={{8,0},{16,8},{24,16},{9,1},{17,9},{25,17},{10,2},{18,10},{26,18},{... | collective-permute-start | bytes 147464 | tf_op jit(solution)/shard_map/ppermute | solution.py:23
  509.2 197.2 %all-reduce.18.cloned.1.call-start = ((), (), s32[]{:S(2)}) async-start(), calls=%async_computation.4 | async-start | bytes 442368 | tf_op jit(solution)/shard_map/psum | solution.py:114
  510.5 162.3 %collective-permute-start.26 = (bf16[48,20,2]{2,0,1:T(8,128)(2,1)S(1)}, bf16[48,20,2]{2,0,1:T(8,128)(2,1)S(1)}, u32[]{:S(2)}, u32[]{:S(2)}) collective-permute-start(bf16[48,20,2]{2,0,1:T(8,128)(2,1)S(1)} %get-tuple-element.148), channel_id=1, source_target_pairs={{0,1},{1,2},{2,3},{3,4},{4,5},{5,6},{6,7},{8,9},{9,10},{10,11},{11... | collective-permute-start | bytes 11528 | tf_op jit(solution)/shard_map/ppermute | solution.py:20
  512.8 160.1 %collective-permute-start.27 = (bf16[48,20,2]{2,0,1:T(8,128)(2,1)S(1)}, bf16[48,20,2]{2,0,1:T(8,128)(2,1)S(1)}, u32[]{:S(2)}, u32[]{:S(2)}) collective-permute-start(bf16[48,20,2]{2,0,1:T(8,128)(2,1)S(1)} %get-tuple-element.149), channel_id=1, source_target_pairs={{1,0},{2,1},{3,2},{4,3},{5,4},{6,5},{7,6},{9,8},{10,9},{11,10},{12... | collective-permute-start | bytes 11528 | tf_op jit(solution)/shard_map/ppermute | solution.py:23
  672.6 231.8 %all-reduce.26.cloned.1.call-start = ((), (), s32[]{:S(2)}) async-start(), calls=%async_computation.8 | async-start | bytes 442368 | tf_op jit(solution)/shard_map/psum | solution.py:103
  777.3 203.2 %all-reduce.22.cloned.1.call-start = ((), (), s32[]{:S(2)}) async-start(), calls=%async_computation.6 | async-start | bytes 442368 | tf_op jit(solution)/shard_map/psum | solution.py:114
  782.5 124.4 %collective-permute-start.32 = (bf16[48,2,256]{0,1,2:T(2,128)(2,1)S(1)}, bf16[48,2,256]{0,1,2:T(2,128)(2,1)S(1)}, u32[]{:S(2)}, u32[]{:S(2)}) collective-permute-start(bf16[48,2,256]{0,1,2:T(2,128)(2,1)S(1)} %get-tuple-element.116), channel_id=1, source_target_pairs={{0,8},{8,16},{16,24},{1,9},{9,17},{17,25},{2,10},{10,18},{18,26},{... | collective-permute-start | bytes 147464 | tf_op jit(solution)/shard_map/ppermute | solution.py:20
  786.1 120.8 %collective-permute-start.33 = (bf16[48,2,256]{0,1,2:T(2,128)(2,1)S(1)}, bf16[48,2,256]{0,1,2:T(2,128)(2,1)S(1)}, u32[]{:S(2)}, u32[]{:S(2)}) collective-permute-start(bf16[48,2,256]{0,1,2:T(2,128)(2,1)S(1)} %get-tuple-element.117), channel_id=1, source_target_pairs={{8,0},{16,8},{24,16},{9,1},{17,9},{25,17},{10,2},{18,10},{26,18},{... | collective-permute-start | bytes 147464 | tf_op jit(solution)/shard_map/ppermute | solution.py:23
  802.6 211.8 %all-reduce.24.cloned.1.call-start = ((), (), s32[]{:S(2)}) async-start(), calls=%async_computation.7 | async-start | bytes 442368 | tf_op jit(solution)/shard_map/psum | solution.py:114
  (82 other events, 1288.6 us)
Sparse Core Ops, SparseCore 0:
  158.6 126.3 all-reduce.13
  289.0 68.8 all-reduce.9
  360.4 31.4 all-reduce.11
  473.0 126.8 all-reduce.19
  603.7 68.8 all-reduce.15
  674.9 31.4 all-reduce.17
  777.4 127.0 all-reduce.25
  908.4 71.9 all-reduce.21
  982.9 31.4 all-reduce.23
